TPU v7x, 512 devices: a whole 4x4x16 slice. The times are simulated.
512 devices in a mesh: term: 8 (over y, core), doc: 16 (over z), enc: 4 (over x).
Axes of the slice: x: 4, y: 4, z: 16, core: 2. Of those that a mesh axis runs over, the one named last changes fastest.
Arguments:
- query_weights: bfloat16 [1024, 30720], P('enc', ('term', 'doc')), may hold values from 0.049804688 to 2
- tile_terms: int32 [30720], P(('term', 'doc')), may hold values from 0 to 59
- tile_blocks: int32 [30720], P(('term', 'doc')), may hold values from 0 to 15
- tile_counts: int32 [128], P(('term', 'doc')), may hold values from 60 to 240, as said below
- impacts: bfloat16 [30720, 64, 128], P(('term', 'doc')), may hold values from -0.015625 to 0.015625
Outputs:
- scores: float32 [2048, 1024], P('doc', 'enc')
Inputs may be any that keep to these rules, and one draw needn't show every extreme that they name: Slots at positions tile_counts or later of a device's list are padding and contribute nothing; some device has all 240 slots live.
All inputs are finite; a program needn't handle non-finite values.
Results may differ from a plain program's by a relative error of at most 0.0003.
Values may be sent and summed in bfloat16 or wider, within the bound.
No kernel may reach another device: no remote copies, remote signals or barrier semaphores. Data moves between devices by JAX's collectives and lax.ppermute only.
A program may use at most 64 MiB of HBM per device.

v0:
```python
import jax
import jax.numpy as jnp
from jax import lax
from jax.sharding import PartitionSpec as P


def block_size(tiles):
    largest = 1
    for divisor in range(1, 65):
        if tiles % divisor == 0:
            largest = divisor
    return largest


def per_device(query_weights, tile_terms, tile_blocks, tile_counts, impacts):
    range_rows = lax.all_gather(query_weights, "doc", axis=1, tiled=True)
    queries = range_rows.shape[0]
    tiles, term_block, doc_block = impacts.shape
    owners = lax.axis_size("doc")
    grouped = range_rows.reshape(queries, range_rows.shape[1] // term_block, term_block)
    step = block_size(tiles)
    live = jnp.arange(tiles, dtype=jnp.int32) < tile_counts[0]
    owner_ids = jnp.arange(owners, dtype=jnp.int32)

    def accumulate(total, number):
        start = number * step
        term_now = lax.dynamic_slice_in_dim(tile_terms, start, step)
        owner_now = lax.dynamic_slice_in_dim(tile_blocks, start, step)
        keep_now = lax.dynamic_slice_in_dim(live, start, step)
        tile_now = lax.dynamic_slice_in_dim(impacts, start, step)
        picked = jnp.take(grouped, term_now, axis=1)
        product = jnp.einsum("qnk,nkd->ndq", picked, tile_now, preferred_element_type=jnp.float32)
        select = ((owner_now[:, None] == owner_ids[None, :]) & keep_now[:, None]).astype(
            jnp.float32
        )
        added = jnp.einsum("ndq,nb->bdq", product, select, precision=lax.Precision.HIGHEST)
        return (total + added, None)

    start_total = jnp.zeros((owners, doc_block, queries), jnp.float32)
    total, unused = lax.scan(accumulate, start_total, jnp.arange(tiles // step, dtype=jnp.int32))
    partial_value = total.reshape(owners * doc_block, queries)
    mine = lax.psum_scatter(partial_value, "doc", scatter_dimension=0, tiled=True)
    scores = lax.psum(mine, "term")
    return scores


def solution(mesh):
    return jax.shard_map(
        per_device,
        mesh=mesh,
        in_specs=(
            P("enc", ("term", "doc")),
            P(("term", "doc")),
            P(("term", "doc")),
            P(("term", "doc")),
            P(("term", "doc"), None, None),
        ),
        out_specs=P("doc", "enc"),
        check_vma=False,
    )
```

profile of v0, /device:TPU:1, one launch (start us, length us, event | category | flops | bytes accessed | tf_op | source)
XLA Modules:
  0.0 312.2 jit_solution(1491762189442942286)
XLA Ops:
  8.0 69.7 %all-gather.2.cloned.1.call-done = bf16[256,3840]{0,1:T(8,128)(2,1)} async-done(((bf16[256,240]{0,1:T(8,128)(2,1)}), bf16[256,3840]{0,1:T(8,128)(2,1)}) %all-gather.2.cloned.1.call-update) | async-done | bytes 1966096 | tf_op jit(solution)/shard_map/all_gather | solution.py:16
  77.7 67.8 %while.11 = (s32[]{:T(128)}, f32[16,128,256]{2,0,1:T(8,128)}, s32[4]{0:T(128)S(1)}, s32[240]{0:T(256)}, pred[240]{0:T(512)(128)(4,1)S(1)}, /*index=5*/bf16[240,6...) while((s32[]{:T(128)}, f32[16,128,256]{2,0,1:T(8,128)}, ...), condition=%wide.region_1.2_spmd.clone, body=%wide.region_0.1_spmd.clone.sunk | while | flops 631180544 | bytes 43587780 | solution.py:40
  79.7 0.8 compare_and_fusion.2
  80.5 2.2 gather_fusion
  82.8 2.6 fusion.28
  85.4 7.9 %select_add_fusion.2 = f32[16,128,256]{2,0,1:T(8,128)S(1)} fusion(f32[16,128,256]{2,0,1:T(8,128)S(1)} %copy-done, f32[60,128,256]{2,1,0:T(8,128)S(1)} %fusion.28, pred[]{:T(512)S(6)} %compare.3, s32[60]{0:T(128)S(1)} %dynamic_slice.31, pred[60]{0:T(512)(128)(4,1)S(1)} %dynamic_slice.32), kind=kOutput, calls=%fused_computation.4.clone.1 | convolution fusion | flops 378537856 | bytes 12058925 | tf_op jit(solution)/shard_map/while/body/eval_jaxpr/ndq,nb->bdq/dot_general | solution.py:36
  93.3 1.3 copy-done.1
  96.7 0.8 compare_and_fusion.2
  97.5 2.2 gather_fusion
  99.7 2.6 fusion.28
  102.3 7.9 %select_add_fusion.2 = f32[16,128,256]{2,0,1:T(8,128)S(1)} fusion(f32[16,128,256]{2,0,1:T(8,128)S(1)} %copy-done, f32[60,128,256]{2,1,0:T(8,128)S(1)} %fusion.28, pred[]{:T(512)S(6)} %compare.3, s32[60]{0:T(128)S(1)} %dynamic_slice.31, pred[60]{0:T(512)(128)(4,1)S(1)} %dynamic_slice.32), kind=kOutput, calls=%fused_computation.4.clone.1 | convolution fusion | flops 378537856 | bytes 12058925 | tf_op jit(solution)/shard_map/while/body/eval_jaxpr/ndq,nb->bdq/dot_general | solution.py:36
  110.2 1.3 copy-done.1
  114.4 2.2 gather_fusion
  116.6 2.6 fusion.28
  119.3 7.9 %select_add_fusion.2 = f32[16,128,256]{2,0,1:T(8,128)S(1)} fusion(f32[16,128,256]{2,0,1:T(8,128)S(1)} %copy-done, f32[60,128,256]{2,1,0:T(8,128)S(1)} %fusion.28, pred[]{:T(512)S(6)} %compare.3, s32[60]{0:T(128)S(1)} %dynamic_slice.31, pred[60]{0:T(512)(128)(4,1)S(1)} %dynamic_slice.32), kind=kOutput, calls=%fused_computation.4.clone.1 | convolution fusion | flops 378537856 | bytes 12058925 | tf_op jit(solution)/shard_map/while/body/eval_jaxpr/ndq,nb->bdq/dot_general | solution.py:36
  127.2 1.3 copy-done.1
  131.3 2.2 gather_fusion
  133.6 2.6 fusion.28
  136.2 7.9 %select_add_fusion.2 = f32[16,128,256]{2,0,1:T(8,128)S(1)} fusion(f32[16,128,256]{2,0,1:T(8,128)S(1)} %copy-done, f32[60,128,256]{2,1,0:T(8,128)S(1)} %fusion.28, pred[]{:T(512)S(6)} %compare.3, s32[60]{0:T(128)S(1)} %dynamic_slice.31, pred[60]{0:T(512)(128)(4,1)S(1)} %dynamic_slice.32), kind=kOutput, calls=%fused_computation.4.clone.1 | convolution fusion | flops 378537856 | bytes 12058925 | tf_op jit(solution)/shard_map/while/body/eval_jaxpr/ndq,nb->bdq/dot_general | solution.py:36
  144.1 1.3 copy-done.1
  145.5 4.1 %copy.8 = f32[16,128,256]{2,1,0:T(8,128)} copy(f32[16,128,256]{2,0,1:T(8,128)} %get-tuple-element.52) | data formatting | bytes 4194304 | tf_op jit(solution)/shard_map/while | solution.py:40
  149.6 69.9 %reduce-scatter.2.cloned.1.call-done = f32[128,256]{1,0:T(8,128)} async-done(((f32[2048,256]{1,0:T(8,128)}), f32[128,256]{1,0:T(8,128)}) %reduce-scatter.2.cloned.1.call-update) | async-done | bytes 131088 | tf_op jit(solution)/shard_map/reduce_scatter | solution.py:42
  219.6 84.5 %all-reduce.2.cloned.1.call-done = f32[128,256]{1,0:T(8,128)} async-done(((f32[128,256]{1,0:T(8,128)}), f32[128,256]{1,0:T(8,128)}) %all-reduce.2.cloned.1.call-update) | async-done | bytes 131088 | tf_op jit(solution)/shard_map/psum | solution.py:43
  304.1 1.6 copy.24
  (39 shorter events, 8.1 us)
Async XLA Ops:
  6.5 71.2 %all-gather.2.cloned.1.call-start = ((), (), s32[]{:S(2)}) async-start(), calls=%async_computation.1 | async-start | bytes 2088960 | tf_op jit(solution)/shard_map/all_gather | solution.py:16
  7.3 212.3 %reduce-scatter.2.cloned.1.call-start = ((), (), s32[]{:S(2)}) async-start(), calls=%async_computation.2 | async-start | bytes 2228224 | tf_op jit(solution)/shard_map/reduce_scatter | solution.py:42
  82.7 2.6 copy-start
  93.3 1.3 copy-start.1
  99.7 2.6 copy-start
  110.2 1.3 copy-start.1
  116.6 2.6 copy-start
  127.2 1.3 copy-start.1
  133.6 2.6 copy-start
  144.1 1.3 copy-start.1
  149.6 154.5 %all-reduce.2.cloned.1.call-start = ((), (), s32[]{:S(2)}) async-start(), calls=%async_computation.3 | async-start | bytes 262144 | tf_op jit(solution)/shard_map/psum | solution.py:43
Sparse Core Ops, SparseCore 0:
  9.4 68.2 all-gather.1
  149.7 69.8 reduce-scatter.1
  221.9 82.1 all-reduce.1
where the time goes:
time: 313 us; the launch traced here: 312 us
  waiting for transfers between devices  225 us (72%)
  matrix products  42 us (13%)
  local copies, waits for them, and re-layouts  25.7 us (8%)
  between operations  13.8 us (4%)
    psum x1, waiting for transfers between devices, per_device(): scores = lax.psum(mine, 'term')  84.5 us
    reduce_scatter x1, waiting for transfers between devices, per_device(): lax.psum_scatter(partial_value, 'doc', scatter_dimension=0, tiled=True)  69.9 us
    all_gather x1, waiting for transfers between devices, per_device(): range_rows = lax.all_gather(query_weights, 'doc', axis=1, tiled=True)  69.7 us
    dot_general x4, matrix products, accumulate(): jnp.einsum('ndq,nb->bdq', product, select, precision=lax.Precision.HIGHEST)  31.6 us
    dot_general x4, matrix products, accumulate(): jnp.einsum('qnk,nkd->ndq', picked, tile_now, preferred_element_type=jnp.f...  10.5 us
    gather x4, local copies, waits for them, and re-layouts, accumulate(): picked = jnp.take(grouped, term_now, axis=1)  8.92 us
  transfers between devices with their start and end apart: 3, of which 3 were waited for; matrix products, arithmetic and copies ran while one was open for 0% of the time, Pallas kernels for 0%

commit v1 on v0

v1 whole, which is shorter than its diff:
```python
import jax
import jax.numpy as jnp
from jax import lax
from jax.experimental import pallas as pl
from jax.experimental.pallas import tpu as pltpu
from jax.sharding import PartitionSpec as P

GROUP = 4
UNROLL = 4


def tile_products(tile_terms, tile_blocks, tile_counts, weights, impacts, parts, owners):
    tiles, term_block, doc_block = impacts.shape
    rows, queries = weights.shape
    zero_block = rows // term_block - 1
    piece = doc_block // parts
    groups = tiles // GROUP + owners + UNROLL
    chunks = 4

    def kernel(terms, blocks, counts, w_ref, tiles_hbm, out_ref, tile_ref, lists, sizes, order, homes, acc, sems):
        share = tiles // chunks
        copies = [
            pltpu.make_async_copy(
                tiles_hbm.at[pl.ds(i * share, share)], tile_ref.at[pl.ds(i * share, share)], sems.at[i]
            )
            for i in range(chunks)
        ]
        for copy in copies:
            copy.start()
        for b in range(owners):
            sizes[b] = 0
        for b in range(owners):
            acc[b] = jnp.zeros((doc_block, queries), jnp.float32)

        def place(j, carry):
            b = blocks[j]
            at = sizes[b]
            lists[b, at] = j + 256 * terms[j]
            sizes[b] = at + 1
            return carry

        lax.fori_loop(0, counts[0], place, 0)

        total = jnp.int32(0)
        for b in range(owners):
            size = sizes[b]
            for k in range(GROUP - 1):
                lists[b, size + k] = 256 * zero_block
            count = lax.div(size + GROUP - 1, GROUP)

            def emit(g, at, b=b):
                for k in range(GROUP):
                    order[at * GROUP + k] = lists[b, g * GROUP + k]
                homes[at] = b
                return at + 1

            total = lax.fori_loop(0, count, emit, total)
        for u in range(UNROLL - 1):
            for k in range(GROUP):
                order[(total + u) * GROUP + k] = 256 * zero_block
            homes[total + u] = 0
        for copy in copies:
            copy.wait()

        def step(s, carry):
            products = []
            for u in range(UNROLL):
                g = s * UNROLL + u
                picked, stacked = [], []
                for k in range(GROUP):
                    entry = order[g * GROUP + k]
                    slot = lax.rem(entry, 256)
                    term = lax.div(entry, 256)
                    stacked.append(tile_ref[slot])
                    picked.append(w_ref[pl.ds(pl.multiple_of(term * term_block, term_block), term_block), :])
                products.append(
                    lax.dot_general(
                        jnp.concatenate(stacked, axis=0),
                        jnp.concatenate(picked, axis=0),
                        (((0,), (0,)), ((), ())),
                        preferred_element_type=jnp.float32,
                    )
                )
            for u in range(UNROLL):
                home = homes[s * UNROLL + u]
                acc[home] += products[u]
            return carry

        lax.fori_loop(0, lax.div(total + UNROLL - 1, UNROLL), step, 0)
        for b in range(owners):
            for p in range(parts):
                out_ref[p, b * piece : (b + 1) * piece, :] = acc[b, p * piece : (p + 1) * piece, :]

    smem = pl.BlockSpec(memory_space=pltpu.SMEM)
    return pl.pallas_call(
        kernel,
        out_shape=jax.ShapeDtypeStruct((parts, owners * piece, queries), jnp.float32),
        in_specs=[smem, smem, smem, pl.BlockSpec(memory_space=pltpu.VMEM), pl.BlockSpec(memory_space=pl.ANY)],
        out_specs=pl.BlockSpec(memory_space=pltpu.VMEM),
        scratch_shapes=[
            pltpu.VMEM((tiles, term_block, doc_block), jnp.bfloat16),
            pltpu.SMEM((owners, tiles + GROUP), jnp.int32),
            pltpu.SMEM((owners,), jnp.int32),
            pltpu.SMEM((groups * GROUP,), jnp.int32),
            pltpu.SMEM((groups,), jnp.int32),
            pltpu.VMEM((owners, doc_block, queries), jnp.float32),
            pltpu.SemaphoreType.DMA((chunks,)),
        ],
        compiler_params=pltpu.CompilerParams(vmem_limit_bytes=40 << 20),
        name="tile_products",
    )(tile_terms, tile_blocks, tile_counts, weights, impacts)


def per_device(query_weights, tile_terms, tile_blocks, tile_counts, impacts):
    parts, owners = lax.axis_size("term"), lax.axis_size("doc")
    doc_block = impacts.shape[2]
    queries = query_weights.shape[0]
    mine = query_weights.T.astype(jnp.float16)
    weights = lax.all_gather(mine, "doc", axis=0, tiled=True).astype(jnp.bfloat16)
    weights = jnp.pad(weights, ((0, impacts.shape[1]), (0, 0)))
    partial = tile_products(tile_terms, tile_blocks, tile_counts, weights, impacts, parts, owners)
    piece = doc_block // parts
    over_term = lax.all_to_all(partial, "term", 0, 0, tiled=True).sum(axis=0)
    over_doc = lax.all_to_all(over_term.reshape(owners, piece, queries), "doc", 0, 0, tiled=True).sum(axis=0)
    return lax.all_gather(over_doc, "term", axis=0, tiled=True)


def solution(mesh):
    return jax.shard_map(
        per_device,
        mesh=mesh,
        in_specs=(
            P("enc", ("term", "doc")),
            P(("term", "doc")),
            P(("term", "doc")),
            P(("term", "doc")),
            P(("term", "doc"), None, None),
        ),
        out_specs=P("doc", "enc"),
        check_vma=False,
    )
```

time: 313 us -> 134 us (0.43)
  waiting for transfers between devices: 225 us -> 0 us
  blocking collectives: 0 us -> 121 us
  matrix products: 42 us -> 0 us
  local copies, waits for them, and re-layouts: 25.7 us -> 2.74 us
  between operations: 13.8 us -> 0.71 us
  Pallas kernels: 0 us -> 7.19 us
    psum x1 -> x0, waiting for transfers between devices: 84.5 us -> none  [per_device(): scores = lax.psum(mine, 'term')]
    reduce_scatter x1 -> x0, waiting for transfers between devices: 69.9 us -> none  [per_device(): lax.psum_scatter(partial_value, 'doc', scatter_dimension=0, tiled=True)]
    all_gather x1 -> x0, waiting for transfers between devices: 69.7 us -> none  [per_device(): range_rows = lax.all_gather(query_weights, 'doc', axis=1, tiled=True)]
    all_gather x0 -> x2, blocking collectives: none -> 62.5 us  [the longest x1 43.3 us: per_device(): lax.all_gather(mine, 'doc', axis=0, tiled=True).astype(jnp.bfloat16)]
    all_to_all x0 -> x2, blocking collectives: none -> 58.9 us  [the longest x1 36.7 us: per_device(): over_term = lax.all_to_all(partial, 'term', 0, 0, tiled=True).sum(axis=0)]
    dot_general x8 -> x0, matrix products: 42 us -> none  [the longest x4 31.6 us: accumulate(): jnp.einsum('ndq,nb->bdq', product, select, precision=lax.Precision.HIGHEST)]
    while x17 -> x0, local copies, waits for them, and re-layouts: 9.5 us -> none
    gather x4 -> x0, local copies, waits for them, and re-layouts: 8.92 us -> none  [accumulate(): picked = jnp.take(grouped, term_now, axis=1)]
  transfers between devices with their start and end apart: 3 -> 0, of which waited for: 3 -> 0; matrix products, arithmetic and copies ran while one was open for 0% -> 0% of each run, Pallas kernels for 0% -> 0%
where the time goes in v1:
time: 134 us
  blocking collectives  121 us (90%)
  Pallas kernels  7.19 us (5%)
  local copies, waits for them, and re-layouts  2.74 us (2%)
  other arithmetic  1.56 us (1%)
    all_gather x1, blocking collectives, per_device(): lax.all_gather(mine, 'doc', axis=0, tiled=True).astype(jnp.bfloat16)  43.3 us
    all_to_all x1, blocking collectives, per_device(): over_term = lax.all_to_all(partial, 'term', 0, 0, tiled=True).sum(axis=0)  36.7 us
    all_to_all x1, blocking collectives, per_device(): lax.all_to_all(over_term.reshape(owners, piece, queries), 'doc', 0, 0, ti...  22.2 us
    all_gather x1, blocking collectives, per_device(): return lax.all_gather(over_doc, 'term', axis=0, tiled=True)  19.2 us
    pallas_call x1, Pallas kernels, tile_products(): pl.pallas_call(kernel, out_shape=jax.ShapeDtypeStruct((parts, owners * pi...  7.19 us

profile of v1, /device:TPU:1, one launch (start us, length us, event | category | flops | bytes accessed | tf_op | source)
XLA Modules:
  0.0 133.6 jit_solution(8237829646185226256)
XLA Ops:
  0.7 0.9 convert_bitcast_fusion
  1.6 43.3 %all-gather.1 = f16[3840,256]{1,0:T(8,128)(2,1)S(1)} all-gather(f16[240,256]{1,0:T(8,128)(2,1)S(1)} %convert_bitcast_fusion), channel_id=1, replica_groups=mesh['term'=8,'doc'=16,'enc'=4] {'doc'}, dimensions={0}, use_global_device_ids=true | all-gather | bytes 2088960 | tf_op jit(solution)/shard_map/all_gather | solution.py:119
  44.9 0.5 convert_element_type.13
  45.4 0.0 copy-start
  45.4 0.0 copy-start.1
  45.4 0.0 copy-start.2
  45.4 0.1 pad.4.w_ref
  45.5 1.9 %copy-done = bf16[240,64,128]{2,1,0:T(8,128)(2,1)S(1)} copy-done((bf16[240,64,128]{2,1,0:T(8,128)(2,1)S(1)}, bf16[240,64,128]{2,1,0:T(8,128)(2,1)}, u32[]{:S(2)}) %copy-start) | copy-done | bytes 3932184
  47.5 0.0 copy-done.1
  47.5 0.0 copy-done.2
  47.5 7.2 %tile_products.1 = f32[8,256,256]{2,1,0:T(8,128)S(1)} custom-call(s32[240]{0:T(256)S(1)} %copy-done.1, s32[240]{0:T(256)S(1)} %copy-done.2, s32[1]{0:T(128)S(6)} %copy.7.counts, bf16[3904,256]{1,0:T(8,128)(2,1)S(1)} %pad.4.w_ref, bf16[240,64,128]{2,1,0:T(8,128)(2,1)S(1)} %copy-done), custom_call_target="tpu_custom_call" | custom-call | tf_op jit(solution)/shard_map/tile_products/pallas_call | solution.py:95
  54.7 36.7 %all_to_all.10 = f32[8,256,256]{2,1,0:T(8,128)S(1)} all-to-all(f32[8,256,256]{2,1,0:T(8,128)S(1)} %tile_products.1), channel_id=1, replica_groups=mesh['term'=8,'doc'=16,'enc'=4] {'term'}, dimensions={0} | all-to-all | bytes 4194304 | tf_op jit(solution)/shard_map/all_to_all | solution.py:123
  91.4 0.1 reduce_sum.18
  91.6 22.2 %all_to_all.11 = f32[16,16,256]{2,1,0:T(8,128)S(1)} all-to-all(f32[16,16,256]{2,1,0:T(8,128)S(1)} %bitcast.3), channel_id=1, replica_groups=mesh['term'=8,'doc'=16,'enc'=4] {'doc'}, dimensions={0} | all-to-all | bytes 524288 | tf_op jit(solution)/shard_map/all_to_all | solution.py:124
  113.8 19.2 %all_gather.7 = f32[128,256]{1,0:T(8,128)S(1)} all-gather(f32[16,256]{1,0:T(8,128)S(1)} %reduce_sum.19), channel_id=1, replica_groups=mesh['term'=8,'doc'=16,'enc'=4] {'term'}, dimensions={0}, use_global_device_ids=true | all-gather | bytes 147456 | tf_op jit(solution)/shard_map/all_gather | solution.py:125
  133.0 0.7 copy.8
  (1 shorter events, 0.0 us)
Async XLA Ops:
  45.4 2.1 %copy-start = (bf16[240,64,128]{2,1,0:T(8,128)(2,1)S(1)}, bf16[240,64,128]{2,1,0:T(8,128)(2,1)}, u32[]{:S(2)}) copy-start(bf16[240,64,128]{2,1,0:T(8,128)(2,1)} %tiles_hbm.1) | copy-start | bytes 11796484
  45.4 2.1 %copy-start.1 = (s32[240]{0:T(256)S(1)}, s32[240]{0:T(256)}, u32[]{:S(2)}) copy-start(s32[240]{0:T(256)} %terms.1) | copy-start | bytes 2884
  45.4 2.1 %copy-start.2 = (s32[240]{0:T(256)S(1)}, s32[240]{0:T(256)}, u32[]{:S(2)}) copy-start(s32[240]{0:T(256)} %blocks.1) | copy-start | bytes 2884

commit v2 on v1

v2 whole, which is shorter than its diff:
```python
import jax
import jax.numpy as jnp
from jax import lax
from jax.experimental import pallas as pl
from jax.experimental.pallas import tpu as pltpu
from jax.sharding import PartitionSpec as P

GROUP = 4
UNROLL = 8
PLACED = 4
STRIDE = 2 * GROUP
CORES = 2
STEPS = (4, 3, 2, 1)
EXTRA = 16


def tile_products(tile_terms, tile_blocks, tile_counts, weights, impacts, parts, owners):
    tiles, term_block, doc_block = impacts.shape
    queries = weights.shape[1]
    piece = doc_block // parts
    groups = tiles // GROUP + owners + UNROLL
    chunks = 4
    nothing = tiles

    def kernel(terms, blocks, counts, w_ref, tiles_hbm, out_ref, tile_ref, state, order, homes, sems):
        share = tiles // chunks
        copies = [
            pltpu.make_async_copy(
                tiles_hbm.at[pl.ds(i * share, share)], tile_ref.at[pl.ds(i * share, share)], sems.at[i]
            )
            for i in range(chunks)
        ]
        for copy in copies:
            copy.start()
        tile_ref[nothing] = jnp.zeros((term_block, doc_block), jnp.bfloat16)
        for p in range(parts):
            out_ref[p] = jnp.zeros((owners * piece, queries), jnp.float32)
        for b in range(owners):
            state[b] = GROUP

        live = counts[0]

        def place(s, total):
            for u in range(PLACED):
                j = s * PLACED + u
                entry = jnp.where(j < live, j + 256 * terms[j], nothing)
                b = blocks[j]
                at = state[b]
                full = (at & (STRIDE - 1)) == GROUP
                at = jnp.where(full, total * STRIDE, at)
                order[at] = entry
                for k in range(1, GROUP):
                    order[at + k] = nothing
                homes[at // STRIDE] = b
                state[b] = at + 1
                total = total + full.astype(jnp.int32)
            return total

        total = lax.fori_loop(0, (live + PLACED - 1) // PLACED, place, jnp.int32(0))
        for u in range(UNROLL - 1):
            for k in range(GROUP):
                order[(total + u) * STRIDE + k] = nothing
            homes[total + u] = 0
        for copy in copies:
            copy.wait()

        def step(s, carry):
            products = []
            for u in range(UNROLL):
                g = s * UNROLL + u
                picked, stacked = [], []
                for k in range(GROUP):
                    entry = order[g * STRIDE + k]
                    stacked.append(tile_ref[entry & 255])
                    row = pl.multiple_of((entry >> 8) * term_block, term_block)
                    picked.append(w_ref[pl.ds(row, term_block), :])
                products.append(
                    lax.dot_general(
                        jnp.concatenate(stacked, axis=0),
                        jnp.concatenate(picked, axis=0),
                        (((0,), (0,)), ((), ())),
                        preferred_element_type=jnp.float32,
                    )
                )
            for u in range(UNROLL):
                row = pl.multiple_of(homes[s * UNROLL + u] * piece, piece)
                for slot in range(parts):
                    p = (slot % (parts // CORES)) * CORES + slot // (parts // CORES)
                    out_ref[slot, pl.ds(row, piece), :] += products[u][p * piece : (p + 1) * piece]
            return carry

        lax.fori_loop(0, (total + UNROLL - 1) // UNROLL, step, 0)

    smem = pl.BlockSpec(memory_space=pltpu.SMEM)
    return pl.pallas_call(
        kernel,
        out_shape=jax.ShapeDtypeStruct((parts, owners * piece, queries), jnp.float32),
        in_specs=[smem, smem, smem, pl.BlockSpec(memory_space=pltpu.VMEM), pl.BlockSpec(memory_space=pltpu.HBM)],
        out_specs=pl.BlockSpec(memory_space=pltpu.VMEM),
        scratch_shapes=[
            pltpu.VMEM((tiles + 1, term_block, doc_block), jnp.bfloat16),
            pltpu.SMEM((owners,), jnp.int32),
            pltpu.SMEM(((groups + 1) * STRIDE,), jnp.int32),
            pltpu.SMEM((groups + 1,), jnp.int32),
            pltpu.SemaphoreType.DMA((chunks,)),
        ],
        compiler_params=pltpu.CompilerParams(vmem_limit_bytes=40 << 20),
        name="tile_products",
    )(tile_terms, tile_blocks, tile_counts, weights, pltpu.with_memory_space_constraint(impacts, pltpu.HBM))


def send(values, axis, groups=None):
    return lax.all_to_all(values, axis, 0, 0, axis_index_groups=groups, tiled=True)


def sum_over_y(values, groups):
    largest = jnp.max(jnp.abs(values))
    level, scale = jnp.float32(0), jnp.float32(1)
    for step in STEPS:
        fits = largest * scale * 2.0 ** (12 * step) <= 32768.0
        level = level + jnp.where(fits, float(step), 0.0)
        scale = scale * jnp.where(fits, 2.0 ** (12 * step), 1.0)
    members, rows, queries = values.shape
    levels = jnp.broadcast_to(level, (members, EXTRA, queries))
    payload = jnp.concatenate([values * scale, levels], axis=1).astype(jnp.float16)
    arrived = send(payload, "term", groups).astype(jnp.float32)
    left = arrived[:, rows : rows + 1, :1]
    back = jnp.ones_like(left)
    for step in STEPS:
        taken = left >= step
        left = left - jnp.where(taken, float(step), 0.0)
        back = back * jnp.where(taken, 2.0 ** (-12 * step), 1.0)
    return (arrived[:, :rows] * back).sum(axis=0)


def per_device(query_weights, tile_terms, tile_blocks, tile_counts, impacts):
    parts, owners = lax.axis_size("term"), lax.axis_size("doc")
    doc_block = impacts.shape[2]
    queries = query_weights.shape[0]
    piece = doc_block // parts
    mine = query_weights.T.astype(jnp.float16)
    weights = lax.all_gather(mine, "doc", axis=0, tiled=True).astype(jnp.bfloat16)
    partial = tile_products(tile_terms, tile_blocks, tile_counts, weights, impacts, parts, owners)
    chips = parts // CORES
    core_groups = [[CORES * y + c for c in range(CORES)] for y in range(chips)]
    y_groups = [[CORES * y + c for y in range(chips)] for c in range(CORES)]
    over_core = send(partial, "term", core_groups).reshape(CORES, chips, owners * piece, queries).sum(axis=0)
    over_term = sum_over_y(over_core, y_groups)
    over_doc = send(over_term.reshape(owners, piece, queries), "doc").sum(axis=0)
    copies = jnp.broadcast_to(over_doc[None], (parts, piece, queries))
    return send(copies, "term").reshape(doc_block, queries)


def solution(mesh):
    return jax.shard_map(
        per_device,
        mesh=mesh,
        in_specs=(
            P("enc", ("term", "doc")),
            P(("term", "doc")),
            P(("term", "doc")),
            P(("term", "doc")),
            P(("term", "doc"), None, None),
        ),
        out_specs=P("doc", "enc"),
        check_vma=False,
    )
```

time: 134 us -> 116 us (0.87)
  blocking collectives: 121 us -> 102 us
  between operations: 0.71 us -> 3.34 us
  local copies, waits for them, and re-layouts: 2.74 us -> 1 us
    all_gather x1 -> x0, blocking collectives: 19.2 us -> none  [per_device(): return lax.all_gather(over_doc, 'term', axis=0, tiled=True)]
    unnamed x7 -> x5, local copies, waits for them, and re-layouts: 2.61 us -> 0.88 us
    all_to_all x2 -> x4, blocking collectives: 58.9 us -> 58.9 us  [send(): lax.all_to_all(values, axis, 0, 0, axis_index_groups=groups, tiled=True)]
where the time goes in v2:
time: 116 us; the launch traced here: 115 us
  blocking collectives  102 us (88%)
  Pallas kernels  6.01 us (5%)
  between operations  3.34 us (3%)
  other arithmetic  2.78 us (2%)
    all_to_all x4, blocking collectives, send(): lax.all_to_all(values, axis, 0, 0, axis_index_groups=groups, tiled=True)  58.9 us
    all_gather x1, blocking collectives, per_device(): lax.all_gather(mine, 'doc', axis=0, tiled=True).astype(jnp.bfloat16)  43.3 us
    pallas_call x1, Pallas kernels, tile_products(): pl.pallas_call(kernel, out_shape=jax.ShapeDtypeStruct((parts, owners * pi...  6.01 us

profile of v2, /device:TPU:1, one launch (start us, length us, event | category | flops | bytes accessed | tf_op | source)
XLA Modules:
  0.0 115.4 jit_solution(11847726938907577114)
XLA Ops:
  0.7 0.9 convert_bitcast_fusion
  1.6 43.3 %all-gather.1 = f16[3840,256]{1,0:T(8,128)(2,1)S(1)} all-gather(f16[240,256]{1,0:T(8,128)(2,1)S(1)} %convert_bitcast_fusion), channel_id=1, replica_groups=mesh['term'=8,'doc'=16,'enc'=4] {'doc'}, dimensions={0}, use_global_device_ids=true | all-gather | bytes 2088960 | tf_op jit(solution)/shard_map/all_gather | solution.py:142
  44.9 0.0 copy-start
  44.9 0.0 copy-start.1
  44.9 0.5 convert_element_type.15.w_ref
  45.4 0.2 copy-done
  45.6 0.0 copy-done.1
  45.6 6.0 %tile_products.1 = f32[8,256,256]{2,1,0:T(8,128)S(1)} custom-call(s32[240]{0:T(256)S(1)} %copy-done, s32[240]{0:T(256)S(1)} %copy-done.1, s32[1]{0:T(128)S(6)} %copy.7.counts, bf16[3840,256]{1,0:T(8,128)(2,1)S(1)} %convert_element_type.15.w_ref, bf16[240,64,128]{2,1,0:T(8,128)(2,1)} %tiles_hbm.1), custom_call_target="tpu_custom_call" | custom-call | tf_op jit(solution)/shard_map/tile_products/pallas_call | solution.py:95
  51.6 11.0 %all_to_all.20 = f32[8,256,256]{2,1,0:T(8,128)S(1)} all-to-all(f32[8,256,256]{2,1,0:T(8,128)S(1)} %tile_products.1), channel_id=1, replica_groups={{0,64},{128,192},{256,320},{384,448},{1,65},{129,193},{257,321},{385,44..., dimensions={0} | all-to-all | bytes 4194304 | tf_op jit(solution)/shard_map/all_to_all | solution.py:113
  62.6 0.2 reduce_sum.27
  62.9 0.7 abs_reduce_fusion
  66.2 0.1 multiply_convert_fusion
  66.3 0.1 concatenate.3
  66.4 14.9 %all_to_all.21 = f16[4,272,256]{2,1,0:T(8,128)(2,1)S(1)} all-to-all(f16[4,272,256]{2,1,0:T(8,128)(2,1)S(1)} %concatenate.3), channel_id=1, replica_groups={{0,128,256,384},{64,192,320,448},{1,129,257,385},{65,193,321,449},{2,13..., dimensions={0} | all-to-all | bytes 1114112 | tf_op jit(solution)/shard_map/all_to_all | solution.py:113
  81.3 0.1 convert_element_type.16
  81.4 0.1 fusion.7
  81.5 0.1 fusion
  81.7 18.5 %all_to_all.22 = f32[16,16,256]{2,1,0:T(8,128)S(1)} all-to-all(f32[16,16,256]{2,1,0:T(8,128)S(1)} %bitcast.6), channel_id=1, replica_groups=mesh['term'=8,'doc'=16,'enc'=4] {'doc'}, dimensions={0} | all-to-all | bytes 524288 | tf_op jit(solution)/shard_map/all_to_all | solution.py:113
  100.2 14.5 %all_to_all.23 = f32[8,16,256]{2,1,0:T(8,128)S(1)} all-to-all(f32[8,16,256]{2,1,0:T(8,128)S(1)} %broadcast_in_dim.41), channel_id=1, replica_groups=mesh['term'=8,'doc'=16,'enc'=4] {'term'}, dimensions={0} | all-to-all | bytes 262144 | tf_op jit(solution)/shard_map/all_to_all | solution.py:113
  114.7 0.7 copy.8
  (2 shorter events, 0.0 us)
Async XLA Ops:
  44.9 0.7 copy-start
  44.9 0.7 copy-start.1

commit v3 on v2

--- a/solution.py
+++ b/solution.py
@@ -14,7 +14,7 @@
 EXTRA = 16
 
 
-def tile_products(tile_terms, tile_blocks, tile_counts, weights, impacts, parts, owners):
+def tile_products(tile_terms, tile_blocks, tile_counts, core, weights, impacts, parts, owners):
     tiles, term_block, doc_block = impacts.shape
     queries = weights.shape[1]
     piece = doc_block // parts
@@ -22,7 +22,7 @@
     chunks = 4
     nothing = tiles
 
-    def kernel(terms, blocks, counts, w_ref, tiles_hbm, out_ref, tile_ref, state, order, homes, sems):
+    def kernel(terms, blocks, counts, core_ref, w_ref, tiles_hbm, out_ref, tile_ref, state, order, homes, sems):
         share = tiles // chunks
         copies = [
             pltpu.make_async_copy(
@@ -84,8 +84,8 @@
                 )
             for u in range(UNROLL):
                 row = pl.multiple_of(homes[s * UNROLL + u] * piece, piece)
-                for slot in range(parts):
-                    p = (slot % (parts // CORES)) * CORES + slot // (parts // CORES)
+                for p in range(parts):
+                    slot = jnp.where(core_ref[0] == p % CORES, 0, parts // CORES) + p // CORES
                     out_ref[slot, pl.ds(row, piece), :] += products[u][p * piece : (p + 1) * piece]
             return carry
 
@@ -95,7 +95,7 @@
     return pl.pallas_call(
         kernel,
         out_shape=jax.ShapeDtypeStruct((parts, owners * piece, queries), jnp.float32),
-        in_specs=[smem, smem, smem, pl.BlockSpec(memory_space=pltpu.VMEM), pl.BlockSpec(memory_space=pltpu.HBM)],
+        in_specs=[smem, smem, smem, smem, pl.BlockSpec(memory_space=pltpu.VMEM), pl.BlockSpec(memory_space=pltpu.HBM)],
         out_specs=pl.BlockSpec(memory_space=pltpu.VMEM),
         scratch_shapes=[
             pltpu.VMEM((tiles + 1, term_block, doc_block), jnp.bfloat16),
@@ -106,7 +106,7 @@
         ],
         compiler_params=pltpu.CompilerParams(vmem_limit_bytes=40 << 20),
         name="tile_products",
-    )(tile_terms, tile_blocks, tile_counts, weights, pltpu.with_memory_space_constraint(impacts, pltpu.HBM))
+    )(tile_terms, tile_blocks, tile_counts, core, weights, pltpu.with_memory_space_constraint(impacts, pltpu.HBM))
 
 
 def send(values, axis, groups=None):
@@ -114,17 +114,17 @@
 
 
 def sum_over_y(values, groups):
-    largest = jnp.max(jnp.abs(values))
-    level, scale = jnp.float32(0), jnp.float32(1)
+    members, rows, queries = values.shape
+    largest = jnp.max(jnp.abs(values), axis=(0, 1))
+    level, scale = jnp.zeros_like(largest), jnp.ones_like(largest)
     for step in STEPS:
         fits = largest * scale * 2.0 ** (12 * step) <= 32768.0
         level = level + jnp.where(fits, float(step), 0.0)
         scale = scale * jnp.where(fits, 2.0 ** (12 * step), 1.0)
-    members, rows, queries = values.shape
     levels = jnp.broadcast_to(level, (members, EXTRA, queries))
     payload = jnp.concatenate([values * scale, levels], axis=1).astype(jnp.float16)
     arrived = send(payload, "term", groups).astype(jnp.float32)
-    left = arrived[:, rows : rows + 1, :1]
+    left = arrived[:, rows : rows + 1, :]
     back = jnp.ones_like(left)
     for step in STEPS:
         taken = left >= step
@@ -140,11 +140,12 @@
     piece = doc_block // parts
     mine = query_weights.T.astype(jnp.float16)
     weights = lax.all_gather(mine, "doc", axis=0, tiled=True).astype(jnp.bfloat16)
-    partial = tile_products(tile_terms, tile_blocks, tile_counts, weights, impacts, parts, owners)
+    core = jnp.reshape(lax.axis_index("term") & (CORES - 1), (1,))
+    partial = tile_products(tile_terms, tile_blocks, tile_counts, core, weights, impacts, parts, owners)
     chips = parts // CORES
-    core_groups = [[CORES * y + c for c in range(CORES)] for y in range(chips)]
     y_groups = [[CORES * y + c for y in range(chips)] for c in range(CORES)]
-    over_core = send(partial, "term", core_groups).reshape(CORES, chips, owners * piece, queries).sum(axis=0)
+    partner = [(i, i ^ 1) for i in range(parts)]
+    over_core = partial[:chips] + lax.ppermute(partial[chips:], "term", partner)
     over_term = sum_over_y(over_core, y_groups)
     over_doc = send(over_term.reshape(owners, piece, queries), "doc").sum(axis=0)
     copies = jnp.broadcast_to(over_doc[None], (parts, piece, queries))

time: 116 us -> 112 us (0.966)
  starting transfers between devices: 0 us -> 12.7 us
  blocking collectives: 102 us -> 89.5 us
  between operations: 3.34 us -> 0.74 us
  waiting for transfers between devices: 0 us -> 2.26 us
  Pallas kernels: 6.01 us -> 4.2 us
    all_to_all x4 -> x3, blocking collectives: 58.9 us -> 46.2 us  [send(): lax.all_to_all(values, axis, 0, 0, axis_index_groups=groups, tiled=True)]
    ppermute x0 -> x1, starting transfers between devices: none -> 12.7 us  [per_device(): over_core = partial[:chips] + lax.ppermute(partial[chips:], 'term', partner)]
    ppermute x0 -> x1, waiting for transfers between devices: none -> 2.26 us  [per_device(): over_core = partial[:chips] + lax.ppermute(partial[chips:], 'term', partner)]
    pallas_call x1, Pallas kernels: 6.01 us -> 4.2 us  [tile_products(): pl.pallas_call(kernel, out_shape=jax.ShapeDtypeStruct((parts, owners * pi...]
  transfers between devices with their start and end apart: 0 -> 1, of which waited for: 0 -> 1; matrix products, arithmetic and copies ran while one was open for 0% -> 0% of each run, Pallas kernels for 0% -> 0%
where the time goes in v3:
time: 112 us
  blocking collectives  89.5 us (80%)
  starting transfers between devices  12.7 us (11%)
  Pallas kernels  4.2 us (4%)
  waiting for transfers between devices  2.26 us (2%)
  other arithmetic  2.03 us (2%)
    all_to_all x3, blocking collectives, send(): lax.all_to_all(values, axis, 0, 0, axis_index_groups=groups, tiled=True)  46.2 us
    all_gather x1, blocking collectives, per_device(): lax.all_gather(mine, 'doc', axis=0, tiled=True).astype(jnp.bfloat16)  43.3 us
    ppermute x1, starting transfers between devices, per_device(): over_core = partial[:chips] + lax.ppermute(partial[chips:], 'term', partner)  12.7 us
    pallas_call x1, Pallas kernels, tile_products(): pl.pallas_call(kernel, out_shape=jax.ShapeDtypeStruct((parts, owners * pi...  4.2 us
    ppermute x1, waiting for transfers between devices, per_device(): over_core = partial[:chips] + lax.ppermute(partial[chips:], 'term', partner)  2.26 us
  transfers between devices with their start and end apart: 1, of which 1 were waited for; matrix products, arithmetic and copies ran while one was open for 0% of the time, Pallas kernels for 0%

profile of v3, /device:TPU:1, one launch (start us, length us, event | category | flops | bytes accessed | tf_op | source)
XLA Modules:
  0.0 112.4 jit_solution(10407306164758747271)
XLA Ops:
  0.7 0.9 convert_bitcast_fusion
  1.6 43.3 %all-gather.1 = f16[3840,256]{1,0:T(8,128)(2,1)S(1)} all-gather(f16[240,256]{1,0:T(8,128)(2,1)S(1)} %convert_bitcast_fusion), channel_id=1, replica_groups=mesh['term'=8,'doc'=16,'enc'=4] {'doc'}, dimensions={0}, use_global_device_ids=true | all-gather | bytes 2088960 | tf_op jit(solution)/shard_map/all_gather | solution.py:142
  44.9 0.0 copy-start
  44.9 0.0 copy-start.1
  44.9 0.5 convert_element_type.15.w_ref
  45.4 0.2 copy-done
  45.6 0.0 copy-done.1
  45.6 4.2 %tile_products.1 = f32[8,256,256]{2,1,0:T(8,128)S(1)} custom-call(s32[240]{0:T(256)S(1)} %copy-done, s32[240]{0:T(256)S(1)} %copy-done.1, s32[1]{0:T(128)S(6)} %copy.10.counts, s32[1]{0:T(128)} %bitcast.core_ref, bf16[3840,256]{1,0:T(8,128)(2,1)S(1)} %convert_element_type.15.w_ref, bf16[240,64,128]{2,1,0:T(8,128)(2,1)} %tiles_hbm.1), custom_call_target="tpu_custom_call" | custom-call | tf_op jit(solution)/shard_map/tile_products/pallas_call | solution.py:95
  49.8 0.1 slice.17
  49.9 12.7 %collective-permute-start = (f32[4,256,256]{2,1,0:T(8,128)S(1)}, f32[4,256,256]{2,1,0:T(8,128)S(1)}, u32[]{:S(2)}, u32[]{:S(2)}) collective-permute-start(f32[4,256,256]{2,1,0:T(8,128)S(1)} %slice.17), channel_id=1, source_target_pairs={{0,64},{64,0},{128,192},{192,128},{256,320},{320,256},{384,448},{4... | collective-permute-start | bytes 3145736 | tf_op jit(solution)/shard_map/ppermute | solution.py:148
  62.6 2.3 %collective-permute-done = f32[4,256,256]{2,1,0:T(8,128)S(1)} collective-permute-done((f32[4,256,256]{2,1,0:T(8,128)S(1)}, f32[4,256,256]{2,1,0:T(8,128)S(1)}, u32[]{:S(2)}, u32[]{:S(2)}) %collective-permute-start) | collective-permute-done | bytes 1048608 | tf_op jit(solution)/shard_map/ppermute | solution.py:148
  64.8 0.1 abs_reduce_fusion
  65.0 0.2 multiply_convert_fusion
  65.2 0.1 pad_maximum_fusion
  65.3 11.8 %all_to_all.15 = f16[4,272,256]{2,1,0:T(8,128)(2,1)S(1)} all-to-all(f16[4,272,256]{2,1,0:T(8,128)(2,1)S(1)} %pad_maximum_fusion), channel_id=1, replica_groups={{0,128,256,384},{64,192,320,448},{1,129,257,385},{65,193,321,449},{2,13..., dimensions={0} | all-to-all | bytes 1114112 | tf_op jit(solution)/shard_map/all_to_all | solution.py:113
  77.1 0.1 convert_element_type.16
  77.2 0.1 fusion
  77.3 19.8 %all_to_all.16 = f32[16,16,256]{2,1,0:T(8,128)S(1)} all-to-all(f32[16,16,256]{2,1,0:T(8,128)S(1)} %bitcast.8), channel_id=1, replica_groups=mesh['term'=8,'doc'=16,'enc'=4] {'doc'}, dimensions={0} | all-to-all | bytes 524288 | tf_op jit(solution)/shard_map/all_to_all | solution.py:113
  97.2 14.5 %all_to_all.17 = f32[8,16,256]{2,1,0:T(8,128)S(1)} all-to-all(f32[8,16,256]{2,1,0:T(8,128)S(1)} %broadcast_in_dim.78), channel_id=1, replica_groups=mesh['term'=8,'doc'=16,'enc'=4] {'term'}, dimensions={0} | all-to-all | bytes 262144 | tf_op jit(solution)/shard_map/all_to_all | solution.py:113
  111.7 0.7 copy.11
  (6 shorter events, 0.1 us)
Async XLA Ops:
  44.9 0.7 copy-start
  44.9 0.7 copy-start.1
  49.9 14.9 %collective-permute-start = (f32[4,256,256]{2,1,0:T(8,128)S(1)}, f32[4,256,256]{2,1,0:T(8,128)S(1)}, u32[]{:S(2)}, u32[]{:S(2)}) collective-permute-start(f32[4,256,256]{2,1,0:T(8,128)S(1)} %slice.17), channel_id=1, source_target_pairs={{0,64},{64,0},{128,192},{192,128},{256,320},{320,256},{384,448},{4... | collective-permute-start | bytes 3145736 | tf_op jit(solution)/shard_map/ppermute | solution.py:148
